TPU v7x, 32 devices: a whole 2x2x4 slice. The times are simulated.
32 devices in a mesh: row: 8 (over z, core), col: 4 (over y, x).
Axes of the slice: x: 2, y: 2, z: 4, core: 2. Of those that a mesh axis runs over, the one named last changes fastest.
Arguments:
- tile_values: bfloat16 [2048, 128, 128], P(('row', 'col')), may hold values from -0.1875 to 0.1875
- slot_codes: int32 [2048], P(('row', 'col')), may hold values from -1 to 127, as said below
- right_start: float32 [8192, 256], P(('row', 'col')), may hold values from -6 to 6
- left_start: float32 [8192, 256], P(('row', 'col')), may hold values from -6 to 6
- node_diagonal: float32 [8192], P(('row', 'col')), may hold values from 1 to 3
- row_scale: float32 [8192], P(('row', 'col')), may hold values from 0.2 to 15
Outputs:
- right_block: float32 [8192, 256], P(('row', 'col'))
- left_block: float32 [8192, 256], P(('row', 'col'))
- projections: float32 [2, 256, 256], replicated
Inputs may be any that keep to these rules, and one draw needn't show every extreme that they name: `slot_codes`: slot (s, p, c) carries a tile that device s extracted for owner p; its code is -1 (empty) or a position a 16 + b in p's block grid of 8 x 2 * 8 places. The codes of one owner's live slots over all sources are distinct, so an owner receives at most 32 live tiles, and some owner receives exactly 32. A source fills at most 2 slots for one owner, and some source fills all 2.
All inputs are finite; a program needn't handle non-finite values.
Results may differ from a plain program's by a relative error of at most 0.002.
Values may be sent and summed in bfloat16 or wider, within the bound.
No kernel may reach another device: no remote copies, remote signals or barrier semaphores. Data moves between devices by JAX's collectives and lax.ppermute only.
A program may use at most 128 MiB of HBM per device.

v0:
```python
import jax
import jax.numpy as jnp
from jax import lax
from jax.sharding import PartitionSpec as P

ITERS = 2
epsilon = 1e-06


def local(tile_values, slot_codes, right_start, left_start, node_diagonal, row_scale):
    row_size = lax.axis_size("row")
    col_size = lax.axis_size("col")
    owners = row_size * col_size
    tile_rows = tile_values.shape[1]
    order_rows = right_start.shape[0] * owners
    grid_rows = 2 * col_size
    grid_cols = 2 * row_size
    got_tiles, got_codes = (
        lax.all_to_all(tile_values, ("row", "col"), split_axis=0, concat_axis=0, tiled=True),
        lax.all_to_all(slot_codes, ("row", "col"), split_axis=0, concat_axis=0, tiled=True),
    )
    live = got_codes >= 0
    places = grid_rows * grid_cols
    safe_keys = jnp.where(live, got_codes, places)
    region = jnp.zeros((places, tile_rows, tile_rows), jnp.bfloat16)
    region = region.at[safe_keys].set(got_tiles, mode="drop")
    region = region.reshape(grid_rows, grid_cols, tile_rows, tile_rows).transpose(0, 2, 1, 3)
    matrix = region.reshape(grid_rows * tile_rows, grid_cols * tile_rows)
    scale_col = row_scale[:, None]
    diag_col = node_diagonal[:, None]
    right_vec = right_start
    left_vec = right_start + left_start
    stored = []
    for turn in range(ITERS):
        right_bf = right_vec.astype(jnp.bfloat16)
        scaled_left = scale_col * left_vec
        left_bf = scaled_left.astype(jnp.bfloat16)
        right_cols = lax.all_gather(right_bf, "row", axis=0, tiled=True)
        left_rows = lax.all_gather(left_bf, "col", axis=0, tiled=True)
        right_part = jnp.dot(matrix, right_cols, preferred_element_type=jnp.float32)
        left_part = lax.dot_general(
            matrix, left_rows, (((0,), (0,)), ((), ())), preferred_element_type=jnp.float32
        )
        right_prod = lax.psum_scatter(right_part, "col", scatter_dimension=0, tiled=True)
        left_prod = lax.psum_scatter(left_part, "row", scatter_dimension=0, tiled=True)
        right_new = scale_col * (right_prod + diag_col * right_vec)
        left_new = left_prod + diag_col * scaled_left
        local_proj = jnp.dot(left_vec.T, right_new, precision=lax.Precision.HIGHEST)
        project = lax.psum(local_proj, ("row", "col")) / order_rows
        right_rest = right_new - jnp.dot(right_vec, project, precision=lax.Precision.HIGHEST)
        left_rest = left_new - jnp.dot(left_vec, project.T, precision=lax.Precision.HIGHEST)
        right_sq, left_sq = lax.psum(
            (jnp.sum(right_rest * right_rest, axis=0), jnp.sum(left_rest * left_rest, axis=0)),
            ("row", "col"),
        )
        right_vec = right_rest / jnp.sqrt(right_sq / order_rows + epsilon)[None, :]
        left_vec = left_rest / jnp.sqrt(left_sq / order_rows + epsilon)[None, :]
        stored.append(project)
    return (right_vec, left_vec, jnp.stack(stored))


def solution(mesh):
    return jax.shard_map(
        local,
        mesh=mesh,
        in_specs=(
            P(("row", "col"), None, None),
            P(("row", "col")),
            P(("row", "col"), None),
            P(("row", "col"), None),
            P(("row", "col")),
            P(("row", "col")),
        ),
        out_specs=(P(("row", "col"), None), P(("row", "col"), None), P()),
        check_vma=False,
    )
```

profile of v0, /device:TPU:10, one launch (start us, length us, event | category | flops | bytes accessed | tf_op | source)
XLA Modules:
  0.0 619.5 jit_solution(10229374278468693904)
XLA Ops:
  7.2 0.0 copy-start.4
  7.2 0.0 copy-start.1
  7.2 0.0 copy-start.3
  7.2 0.8 all_to_all.11
  8.0 10.9 %all_to_all.17 = s32[32,2,1]{1,2,0:T(1,128)S(1)} all-to-all(s32[32,2,1]{1,2,0:T(1,128)S(1)} %bitcast.37), channel_id=1, replica_groups=mesh['row'=8,'col'=4] {'row','col'}, dimensions={0} | all-to-all | bytes 512 | tf_op jit(solution)/shard_map/all_to_all | solution.py:20
  18.9 4.8 all-to-all-start.1
  23.7 0.0 all-gather.3.cloned.1.call-start
  23.8 0.0 copy-done.4
  23.8 0.0 copy-done.1
  23.8 0.0 copy-done.3
  23.8 0.7 multiply_convert_fusion.1
  24.5 0.0 all-gather.3.cloned.1.call-update
  24.5 0.0 reduce-scatter.5.cloned.1.call-start
  24.6 0.5 broadcast.86
  25.1 0.7 reduce.3
  25.8 0.1 all_to_all.13
  25.9 51.8 %all-to-all-done.1 = bf16[64,128,128]{2,1,0:T(8,128)(2,1)S(1)} async-done(((bf16[64,128,128]{2,1,0:T(8,128)(2,1)}), bf16[64,128,128]{2,1,0:T(8,128)(2,1)S(1)}, u32[]{:S(2)}, u32[]{:S(2)}) %all-to-all-start.1) | async-done | bytes 2097184 | tf_op jit(solution)/shard_map/all_to_all | solution.py:19
  77.7 3.0 broadcast_in_dim.6
  80.7 10.7 %scatter_fusion = bf16[128,128,128]{2,1,0:T(8,128)(2,1)} fusion(bf16[128,128,128]{2,1,0:T(8,128)(2,1)} %broadcast_in_dim.6, s32[64]{0:T(128)S(1)} %fusion.27, bf16[64,128,128]{2,1,0:T(8,128)(2,1)S(1)} %all-to-all-done.1), kind=kCustom, calls=%fused_computation | custom fusion | bytes 6291712 | tf_op jit(solution)/shard_map/scatter | solution.py:26
  91.4 6.8 %copy.11 = bf16[8,16,128,128]{3,1,2,0:T(8,128)(2,1)} copy(bf16[8,16,128,128]{3,2,1,0:T(8,128)(2,1)} %bitcast.32) | data formatting | bytes 8388608 | tf_op jit(solution)/shard_map/reshape | solution.py:27
  98.3 4.7 fusion.6
  103.0 0.0 reduce-scatter.5.cloned.1.call-update
  103.0 0.0 all-reduce.5.cloned.1.call-start
  103.1 15.5 %all_gather.14 = bf16[1024,256]{1,0:T(8,128)(2,1)S(1)} all-gather(bf16[256,256]{1,0:T(8,128)(2,1)S(1)} %get-tuple-element.7), channel_id=1, replica_groups=mesh['row'=8,'col'=4] {'col'}, dimensions={0}, use_global_device_ids=true | all-gather | bytes 655360 | tf_op jit(solution)/shard_map/all_gather | solution.py:39
  118.6 15.7 %reduce-scatter.5.cloned.1.call-done = f32[256,256]{1,0:T(8,128)} async-done(((f32[1024,256]{1,0:T(8,128)}), f32[256,256]{1,0:T(8,128)}) %reduce-scatter.5.cloned.1.call-update) | async-done | bytes 262160 | tf_op jit(solution)/shard_map/reduce_scatter | solution.py:44
  134.3 0.0 copy-done.5
  134.3 2.3 fusion.17
  136.6 0.0 all-reduce.5.cloned.1.call-update
  136.6 0.0 copy-start.2
  136.6 0.0 reduce-scatter.9.cloned.1.call-start
  136.7 5.6 fusion.2
  142.3 0.0 reduce-scatter.9.cloned.1.call-update
  142.3 0.0 all-gather.5.cloned.1.call-start
  142.3 124.6 %all-reduce.5.cloned.1.call-done = f32[256,256]{1,0:T(8,128)} async-done(((f32[256,256]{1,0:T(8,128)}), f32[256,256]{1,0:T(8,128)}) %all-reduce.5.cloned.1.call-update) | async-done | bytes 262160 | tf_op jit(solution)/shard_map/psum | solution.py:49
  266.9 0.0 copy-done.2
  266.9 1.4 multiply_reduce_fusion.3
  268.3 32.0 %reduce-scatter.9.cloned.1.call-done = f32[256,256]{1,0:T(8,128)} async-done(((f32[2048,256]{1,0:T(8,128)}), f32[256,256]{1,0:T(8,128)}) %reduce-scatter.9.cloned.1.call-update) | async-done | bytes 262160 | tf_op jit(solution)/shard_map/reduce_scatter | solution.py:45
  300.4 1.5 multiply_reduce_fusion.2
  301.8 43.8 %all-reduce.1 = (f32[256]{0:T(256)S(1)}, f32[256]{0:T(256)S(1)}) all-reduce(f32[256]{0:T(256)S(1)} %get-tuple-element.10, f32[256]{0:T(256)S(1)} %get-tuple-element.12), channel_id=1, replica_groups=mesh['row'=8,'col'=4] {'row','col'}, use_global_device_ids=true, to_apply=%region_4.5 | all-reduce | flops 512 | bytes 4096 | tf_op jit(solution)/shard_map/psum | solution.py:52
  345.6 0.7 fusion.32
  346.3 0.0 all-gather.5.cloned.1.call-update
  346.3 0.2 reduce-scatter.7.cloned.1.call-start
  346.5 20.5 %all-gather.5.cloned.1.call-done = bf16[2048,256]{1,0:T(8,128)(2,1)} async-done(((bf16[256,256]{1,0:T(8,128)(2,1)}), bf16[2048,256]{1,0:T(8,128)(2,1)}) %all-gather.5.cloned.1.call-update) | async-done | bytes 1048592 | tf_op jit(solution)/shard_map/all_gather | solution.py:38
  367.1 4.7 fusion.4
  371.8 0.0 reduce-scatter.7.cloned.1.call-update
  371.8 0.0 all-reduce.7.cloned.1.call-start
  371.9 0.1 multiply_convert_fusion
  372.0 13.6 %all_gather.15 = bf16[1024,256]{1,0:T(8,128)(2,1)S(1)} all-gather(bf16[256,256]{1,0:T(8,128)(2,1)S(1)} %multiply_convert_fusion), channel_id=1, replica_groups=mesh['row'=8,'col'=4] {'col'}, dimensions={0}, use_global_device_ids=true | all-gather | bytes 655360 | tf_op jit(solution)/shard_map/all_gather | solution.py:39
  385.6 14.1 %reduce-scatter.7.cloned.1.call-done = f32[256,256]{1,0:T(8,128)} async-done(((f32[1024,256]{1,0:T(8,128)}), f32[256,256]{1,0:T(8,128)}) %reduce-scatter.7.cloned.1.call-update) | async-done | bytes 262160 | tf_op jit(solution)/shard_map/reduce_scatter | solution.py:44
  399.7 2.3 fusion.18
  402.0 0.0 all-reduce.7.cloned.1.call-update
  402.0 0.0 copy-start
  402.1 0.0 reduce-scatter.11.cloned.1.call-start
  402.1 5.6 fusion
  407.7 0.0 reduce-scatter.11.cloned.1.call-update
  407.7 124.6 %all-reduce.7.cloned.1.call-done = f32[256,256]{1,0:T(8,128)} async-done(((f32[256,256]{1,0:T(8,128)}), f32[256,256]{1,0:T(8,128)}) %all-reduce.7.cloned.1.call-update) | async-done | bytes 262160 | tf_op jit(solution)/shard_map/psum | solution.py:49
  532.4 1.0 multiply_bitcast_fusion
  533.3 0.8 pad_maximum_fusion
  534.2 1.4 multiply_reduce_fusion.1
  535.5 30.5 %reduce-scatter.11.cloned.1.call-done = f32[256,256]{1,0:T(8,128)} async-done(((f32[2048,256]{1,0:T(8,128)}), f32[256,256]{1,0:T(8,128)}) %reduce-scatter.11.cloned.1.call-update) | async-done | bytes 262160 | tf_op jit(solution)/shard_map/reduce_scatter | solution.py:45
  566.1 1.5 multiply_reduce_fusion
  567.5 43.6 %all-reduce = (f32[256]{0:T(256)S(1)}, f32[256]{0:T(256)S(1)}) all-reduce(f32[256]{0:T(256)S(1)} %get-tuple-element.14, f32[256]{0:T(256)S(1)} %get-tuple-element.16), channel_id=1, replica_groups=mesh['row'=8,'col'=4] {'row','col'}, use_global_device_ids=true, to_apply=%region_11.12 | all-reduce | flops 512 | bytes 4096 | tf_op jit(solution)/shard_map/psum | solution.py:52
  611.2 0.7 broadcast_divide_fusion
  611.9 0.7 broadcast_divide_fusion.1
  (10 shorter events, 0.1 us)
Async XLA Ops:
  7.2 16.6 %copy-start.4 = (f32[256]{0:T(256)S(1)}, f32[256]{0:T(256)}, u32[]{:S(2)}) copy-start(f32[256]{0:T(256)} %param.11) | copy-start | bytes 3076
  7.2 16.6 %copy-start.1 = (f32[256,256]{1,0:T(8,128)S(1)}, f32[256,256]{1,0:T(8,128)}, u32[]{:S(2)}) copy-start(f32[256,256]{1,0:T(8,128)} %param.8) | copy-start | bytes 786436
  7.2 16.6 %copy-start.3 = (f32[256,256]{1,0:T(8,128)S(1)}, f32[256,256]{1,0:T(8,128)}, u32[]{:S(2)}) copy-start(f32[256,256]{1,0:T(8,128)} %param.9) | copy-start | bytes 786436
  18.9 58.8 %all-to-all-start.1 = ((bf16[64,128,128]{2,1,0:T(8,128)(2,1)}), bf16[64,128,128]{2,1,0:T(8,128)(2,1)S(1)}, u32[]{:S(2)}, u32[]{:S(2)}) async-start(bf16[64,128,128]{2,1,0:T(8,128)(2,1)} %param.6), calls=%async_computation.1 | async-start | bytes 4194304 | tf_op jit(solution)/shard_map/all_to_all | solution.py:19
  23.7 74.6 %all-gather.3.cloned.1.call-start = ((), (), s32[]{:S(2)}) async-start(), calls=%async_computation.6 | async-start | bytes 1179648 | tf_op jit(solution)/shard_map/all_gather | solution.py:38
  24.5 109.7 %reduce-scatter.5.cloned.1.call-start = ((), (), s32[]{:S(2)}) async-start(), calls=%async_computation.7 | async-start | bytes 1310720 | tf_op jit(solution)/shard_map/reduce_scatter | solution.py:44
  98.3 36.0 %copy-start.5 = (f32[256]{0:T(256)S(1)}, f32[256]{0:T(256)}, u32[]{:S(2)}) copy-start(f32[256]{0:T(256)} %param.10) | copy-start | bytes 3076
  103.0 163.9 %all-reduce.5.cloned.1.call-start = ((), (), s32[]{:S(2)}) async-start(), calls=%async_computation.8 | async-start | bytes 524288 | tf_op jit(solution)/shard_map/psum | solution.py:49
  136.6 130.3 %copy-start.2 = (f32[256,256]{1,0:T(8,128)S(1)}, f32[256,256]{1,0:T(8,128)}, u32[]{:S(2)}) copy-start(f32[256,256]{1,0:T(8,128)} %reduce-scatter.5.cloned.1.call-done) | copy-start | bytes 786436
  136.6 163.7 %reduce-scatter.9.cloned.1.call-start = ((), (), s32[]{:S(2)}) async-start(), calls=%async_computation.11 | async-start | bytes 2359296 | tf_op jit(solution)/shard_map/reduce_scatter | solution.py:45
  142.3 224.8 %all-gather.5.cloned.1.call-start = ((), (), s32[]{:S(2)}) async-start(), calls=%async_computation.9 | async-start | bytes 1179648 | tf_op jit(solution)/shard_map/all_gather | solution.py:38
  346.3 53.4 %reduce-scatter.7.cloned.1.call-start = ((), (), s32[]{:S(2)}) async-start(), calls=%async_computation.10 | async-start | bytes 1310720 | tf_op jit(solution)/shard_map/reduce_scatter | solution.py:44
  371.8 160.6 %all-reduce.7.cloned.1.call-start = ((), (), s32[]{:S(2)}) async-start(), calls=%async_computation.12 | async-start | bytes 524288 | tf_op jit(solution)/shard_map/psum | solution.py:49
  402.0 5.7 copy-start
  402.1 164.0 %reduce-scatter.11.cloned.1.call-start = ((), (), s32[]{:S(2)}) async-start(), calls=%async_computation.13 | async-start | bytes 2359296 | tf_op jit(solution)/shard_map/reduce_scatter | solution.py:45
  407.7 126.5 %copy-start.6 = (f32[256,256]{1,0:T(8,128)S(1)}, f32[256,256]{1,0:T(8,128)}, u32[]{:S(2)}) copy-start(f32[256,256]{1,0:T(8,128)} %reduce-scatter.7.cloned.1.call-done) | copy-start | bytes 786436
Sparse Core Ops, SparseCore 0:
  26.7 30.5 all-gather.2
  103.2 31.0 reduce-scatter.4
  140.3 126.5 all-reduce.4
  269.1 31.2 reduce-scatter.8
  346.4 20.5 all-gather.4
  371.9 27.7 reduce-scatter.6
  405.8 126.5 all-reduce.6
  534.7 31.3 reduce-scatter.10
where the time goes:
time: 621 us; the launch traced here: 619 us
  waiting for transfers between devices  414 us (67%)
  blocking collectives  127 us (20%)
  matrix products  30.9 us (5%)
  local copies, waits for them, and re-layouts  22 us (4%)
  between operations  14.3 us (2%)
    psum x2, waiting for transfers between devices, local(): project = lax.psum(local_proj, ('row', 'col')) / order_rows  249 us
    psum x2, blocking collectives, local(): lax.psum((jnp.sum(right_rest * right_rest, axis=0), jnp.sum(left_rest * l...  87.4 us
    reduce_scatter x2, waiting for transfers between devices, local(): lax.psum_scatter(left_part, 'row', scatter_dimension=0, tiled=True)  62.6 us
    all_to_all x1, waiting for transfers between devices, local(): lax.all_to_all(tile_values, ('row', 'col'), split_axis=0, concat_axis=0,...  51.8 us
    reduce_scatter x2, waiting for transfers between devices, local(): lax.psum_scatter(right_part, 'col', scatter_dimension=0, tiled=True)  29.8 us
    all_gather x2, blocking collectives, local(): left_rows = lax.all_gather(left_bf, 'col', axis=0, tiled=True)  29.1 us
    all_gather x2, waiting for transfers between devices, local(): right_cols = lax.all_gather(right_bf, 'row', axis=0, tiled=True)  20.5 us
  transfers between devices with their start and end apart: 9, of which 8 were waited for; matrix products, arithmetic and copies ran while one was open for 6% of the time, Pallas kernels for 0%

commit v1 on v0

--- a/solution.py
+++ b/solution.py
@@ -46,7 +46,7 @@
         right_new = scale_col * (right_prod + diag_col * right_vec)
         left_new = left_prod + diag_col * scaled_left
         local_proj = jnp.dot(left_vec.T, right_new, precision=lax.Precision.HIGHEST)
-        project = lax.psum(local_proj, ("row", "col")) / order_rows
+        project = lax.all_gather(local_proj, ("row", "col")).sum(axis=0) / order_rows
         right_rest = right_new - jnp.dot(right_vec, project, precision=lax.Precision.HIGHEST)
         left_rest = left_new - jnp.dot(left_vec, project.T, precision=lax.Precision.HIGHEST)
         right_sq, left_sq = lax.psum(

time: 621 us -> 513 us (0.83)
  waiting for transfers between devices: 414 us -> 313 us
  blocking collectives: 127 us -> 117 us
  other arithmetic: 5.48 us -> 12.5 us
    psum x2 -> x0, waiting for transfers between devices: 249 us -> none  [local(): project = lax.psum(local_proj, ('row', 'col')) / order_rows]
    all_gather x0 -> x2, waiting for transfers between devices: none -> 126 us  [local(): lax.all_gather(local_proj, ('row', 'col')).sum(axis=0) / order_rows]
    reduce_scatter x2, waiting for transfers between devices: 29.8 us -> 57.8 us  [local(): lax.psum_scatter(right_part, 'col', scatter_dimension=0, tiled=True)]
    all_gather x2, blocking collectives: 29.1 us -> 18.2 us  [local(): left_rows = lax.all_gather(left_bf, 'col', axis=0, tiled=True)]
    reduce_sum x0 -> x2, other arithmetic: none -> 7.94 us  [local(): lax.all_gather(local_proj, ('row', 'col')).sum(axis=0) / order_rows]
  transfers between devices with their start and end apart: 9 -> 9, of which waited for: 8 -> 8; matrix products, arithmetic and copies ran while one was open for 6% -> 8% of each run, Pallas kernels for 0% -> 0%
where the time goes in v1:
time: 513 us; the launch traced here: 512 us
  waiting for transfers between devices  313 us (61%)
  blocking collectives  117 us (23%)
  matrix products  29.2 us (6%)
  local copies, waits for them, and re-layouts  20.5 us (4%)
  between operations  14.3 us (3%)
  other arithmetic  12.5 us (2%)
  starting transfers between devices  5.32 us (1%)
    all_gather x2, waiting for transfers between devices, local(): lax.all_gather(local_proj, ('row', 'col')).sum(axis=0) / order_rows  126 us
    psum x2, blocking collectives, local(): lax.psum((jnp.sum(right_rest * right_rest, axis=0), jnp.sum(left_rest * l...  87.5 us
    reduce_scatter x2, waiting for transfers between devices, local(): lax.psum_scatter(right_part, 'col', scatter_dimension=0, tiled=True)  57.8 us
    reduce_scatter x2, waiting for transfers between devices, local(): lax.psum_scatter(left_part, 'row', scatter_dimension=0, tiled=True)  56.6 us
    all_to_all x1, waiting for transfers between devices, local(): lax.all_to_all(tile_values, ('row', 'col'), split_axis=0, concat_axis=0,...  51.8 us
    all_gather x2, waiting for transfers between devices, local(): right_cols = lax.all_gather(right_bf, 'row', axis=0, tiled=True)  20.6 us
    all_gather x2, blocking collectives, local(): left_rows = lax.all_gather(left_bf, 'col', axis=0, tiled=True)  18.2 us
    dot_general x2, matrix products, local(): lax.dot_general(matrix, left_rows, (((0,), (0,)), ((), ())), preferred_el...  11.5 us
  transfers between devices with their start and end apart: 9, of which 8 were waited for; matrix products, arithmetic and copies ran while one was open for 8% of the time, Pallas kernels for 0%

profile of v1, /device:TPU:10, one launch (start us, length us, event | category | flops | bytes accessed | tf_op | source)
XLA Modules:
  0.0 511.7 jit_solution(10641434819742502461)
XLA Ops:
  7.2 0.0 copy-start.3
  7.2 0.0 copy-start
  7.2 0.0 copy-start.2
  7.2 0.8 all_to_all.11
  8.0 10.9 %all_to_all.17 = s32[32,2,1]{1,2,0:T(1,128)S(1)} all-to-all(s32[32,2,1]{1,2,0:T(1,128)S(1)} %bitcast.41), channel_id=1, replica_groups=mesh['row'=8,'col'=4] {'row','col'}, dimensions={0} | all-to-all | bytes 512 | tf_op jit(solution)/shard_map/all_to_all | solution.py:20
  18.9 4.8 all-to-all-start.1
  23.7 0.0 all-gather.7.cloned.1.call-start
  23.8 0.0 copy-done.3
  23.8 0.0 copy-done
  23.8 0.0 copy-done.2
  23.8 0.7 multiply_convert_fusion.1
  24.5 0.0 all-gather.7.cloned.1.call-update
  24.5 0.0 reduce-scatter.5.cloned.1.call-start
  24.6 0.5 broadcast.103
  25.1 0.7 reduce.3
  25.8 0.1 all_to_all.13
  25.9 51.8 %all-to-all-done.1 = bf16[64,128,128]{2,1,0:T(8,128)(2,1)S(1)} async-done(((bf16[64,128,128]{2,1,0:T(8,128)(2,1)}), bf16[64,128,128]{2,1,0:T(8,128)(2,1)S(1)}, u32[]{:S(2)}, u32[]{:S(2)}) %all-to-all-start.1) | async-done | bytes 2097184 | tf_op jit(solution)/shard_map/all_to_all | solution.py:19
  77.7 3.0 broadcast_in_dim.6
  80.7 9.2 %scatter_fusion = bf16[128,128,128]{2,1,0:T(8,128)(2,1)} fusion(bf16[128,128,128]{2,1,0:T(8,128)(2,1)} %broadcast_in_dim.6, s32[64]{0:T(128)S(1)} %fusion.27, bf16[64,128,128]{2,1,0:T(8,128)(2,1)S(1)} %all-to-all-done.1), kind=kCustom, calls=%fused_computation | custom fusion | bytes 6291712 | tf_op jit(solution)/shard_map/scatter | solution.py:26
  89.9 6.9 %copy.11 = bf16[8,16,128,128]{3,1,2,0:T(8,128)(2,1)} copy(bf16[8,16,128,128]{3,2,1,0:T(8,128)(2,1)} %bitcast.34) | data formatting | bytes 8388608 | tf_op jit(solution)/shard_map/reshape | solution.py:27
  96.8 4.8 fusion.6
  101.5 0.0 reduce-scatter.5.cloned.1.call-update
  101.5 0.0 all-gather.11.cloned.1.call-start
  101.6 30.3 %reduce-scatter.5.cloned.1.call-done = f32[256,256]{1,0:T(8,128)} async-done(((f32[1024,256]{1,0:T(8,128)}), f32[256,256]{1,0:T(8,128)}) %reduce-scatter.5.cloned.1.call-update) | async-done | bytes 262160 | tf_op jit(solution)/shard_map/reduce_scatter | solution.py:44
  131.9 0.0 copy-done.4
  131.9 2.3 fusion.17
  134.3 0.0 all-gather.11.cloned.1.call-update
  134.3 0.0 reduce-scatter.9.cloned.1.call-start
  134.3 9.1 %all_gather.28 = bf16[1024,256]{1,0:T(8,128)(2,1)S(1)} all-gather(bf16[256,256]{1,0:T(8,128)(2,1)S(1)} %get-tuple-element.7), channel_id=1, replica_groups=mesh['row'=8,'col'=4] {'col'}, dimensions={0}, use_global_device_ids=true | all-gather | bytes 655360 | tf_op jit(solution)/shard_map/all_gather | solution.py:39
  143.4 5.7 %fusion.2 = f32[2048,256]{1,0:T(8,128)} fusion(bf16[1024,256]{1,0:T(8,128)(2,1)S(1)} %all_gather.28, bf16[128,8,16,128]{3,2,1,0:T(8,128)(2,1)} %bitcast.38), kind=kOutput, calls=%fused_computation.3 | convolution fusion | flops 1073741824 | bytes 6815744 | tf_op jit(solution)/shard_map/dot_general | solution.py:41
  149.1 0.0 reduce-scatter.9.cloned.1.call-update
  149.2 0.0 all-gather.9.cloned.1.call-start
  149.2 63.2 %all-gather.11.cloned.1.call-done = f32[8192,256]{1,0:T(8,128)} async-done(((f32[256,256]{1,0:T(8,128)}), f32[8192,256]{1,0:T(8,128)}) %all-gather.11.cloned.1.call-update) | async-done | bytes 8388624 | tf_op jit(solution)/shard_map/all_gather | solution.py:49
  212.5 4.0 reduce_sum.54
  216.4 0.0 copy-done.1
  216.4 0.4 multiply_reduce_fusion.3
  216.9 28.7 %reduce-scatter.9.cloned.1.call-done = f32[256,256]{1,0:T(8,128)} async-done(((f32[2048,256]{1,0:T(8,128)}), f32[256,256]{1,0:T(8,128)}) %reduce-scatter.9.cloned.1.call-update) | async-done | bytes 262160 | tf_op jit(solution)/shard_map/reduce_scatter | solution.py:45
  245.5 1.4 multiply_reduce_fusion.2
  246.9 43.8 %all-reduce.1 = (f32[256]{0:T(256)S(1)}, f32[256]{0:T(256)S(1)}) all-reduce(f32[256]{0:T(256)S(1)} %get-tuple-element.10, f32[256]{0:T(256)S(1)} %get-tuple-element.12), channel_id=1, replica_groups=mesh['row'=8,'col'=4] {'row','col'}, use_global_device_ids=true, to_apply=%region_4.5 | all-reduce | flops 512 | bytes 4096 | tf_op jit(solution)/shard_map/psum | solution.py:52
  290.7 0.7 fusion.32
  291.4 0.0 all-gather.9.cloned.1.call-update
  291.4 0.2 reduce-scatter.7.cloned.1.call-start
  291.6 20.6 %all-gather.9.cloned.1.call-done = bf16[2048,256]{1,0:T(8,128)(2,1)} async-done(((bf16[256,256]{1,0:T(8,128)(2,1)}), bf16[2048,256]{1,0:T(8,128)(2,1)}) %all-gather.9.cloned.1.call-update) | async-done | bytes 1048592 | tf_op jit(solution)/shard_map/all_gather | solution.py:38
  312.2 4.7 fusion.4
  317.0 0.0 reduce-scatter.7.cloned.1.call-update
  317.0 0.0 all-gather.13.cloned.1.call-start
  317.0 27.5 %reduce-scatter.7.cloned.1.call-done = f32[256,256]{1,0:T(8,128)} async-done(((f32[1024,256]{1,0:T(8,128)}), f32[256,256]{1,0:T(8,128)}) %reduce-scatter.7.cloned.1.call-update) | async-done | bytes 262160 | tf_op jit(solution)/shard_map/reduce_scatter | solution.py:44
  344.6 2.3 fusion.18
  346.9 0.0 all-gather.13.cloned.1.call-update
  346.9 0.0 reduce-scatter.11.cloned.1.call-start
  347.0 0.1 multiply_convert_fusion
  347.1 9.1 %all_gather.31 = bf16[1024,256]{1,0:T(8,128)(2,1)S(1)} all-gather(bf16[256,256]{1,0:T(8,128)(2,1)S(1)} %multiply_convert_fusion), channel_id=1, replica_groups=mesh['row'=8,'col'=4] {'col'}, dimensions={0}, use_global_device_ids=true | all-gather | bytes 655360 | tf_op jit(solution)/shard_map/all_gather | solution.py:39
  356.2 5.7 %fusion = f32[2048,256]{1,0:T(8,128)} fusion(bf16[1024,256]{1,0:T(8,128)(2,1)S(1)} %all_gather.31, bf16[128,8,16,128]{3,2,1,0:T(8,128)(2,1)} %bitcast.40), kind=kOutput, calls=%fused_computation.1 | convolution fusion | flops 1073741824 | bytes 6815744 | tf_op jit(solution)/shard_map/dot_general | solution.py:41
  361.9 0.0 reduce-scatter.11.cloned.1.call-update
  361.9 63.1 %all-gather.13.cloned.1.call-done = f32[8192,256]{1,0:T(8,128)} async-done(((f32[256,256]{1,0:T(8,128)}), f32[8192,256]{1,0:T(8,128)}) %all-gather.13.cloned.1.call-update) | async-done | bytes 8388624 | tf_op jit(solution)/shard_map/all_gather | solution.py:49
  425.1 4.0 reduce_sum.57
  429.1 0.8 pad_maximum_fusion
  429.9 0.0 copy-done.5
  429.9 0.4 multiply_reduce_fusion.1
  430.3 28.0 %reduce-scatter.11.cloned.1.call-done = f32[256,256]{1,0:T(8,128)} async-done(((f32[2048,256]{1,0:T(8,128)}), f32[256,256]{1,0:T(8,128)}) %reduce-scatter.11.cloned.1.call-update) | async-done | bytes 262160 | tf_op jit(solution)/shard_map/reduce_scatter | solution.py:45
  458.3 1.4 multiply_reduce_fusion
  459.7 43.8 %all-reduce = (f32[256]{0:T(256)S(1)}, f32[256]{0:T(256)S(1)}) all-reduce(f32[256]{0:T(256)S(1)} %get-tuple-element.14, f32[256]{0:T(256)S(1)} %get-tuple-element.16), channel_id=1, replica_groups=mesh['row'=8,'col'=4] {'row','col'}, use_global_device_ids=true, to_apply=%region_11.12 | all-reduce | flops 512 | bytes 4096 | tf_op jit(solution)/shard_map/psum | solution.py:52
  503.4 0.7 broadcast_divide_fusion
  504.2 0.7 broadcast_divide_fusion.1
  (10 shorter events, 0.1 us)
Async XLA Ops:
  7.2 16.6 %copy-start.3 = (f32[256]{0:T(256)S(1)}, f32[256]{0:T(256)}, u32[]{:S(2)}) copy-start(f32[256]{0:T(256)} %param.11) | copy-start | bytes 3076
  7.2 16.6 %copy-start = (f32[256,256]{1,0:T(8,128)S(1)}, f32[256,256]{1,0:T(8,128)}, u32[]{:S(2)}) copy-start(f32[256,256]{1,0:T(8,128)} %param.8) | copy-start | bytes 786436
  7.2 16.6 %copy-start.2 = (f32[256,256]{1,0:T(8,128)S(1)}, f32[256,256]{1,0:T(8,128)}, u32[]{:S(2)}) copy-start(f32[256,256]{1,0:T(8,128)} %param.9) | copy-start | bytes 786436
  18.9 58.8 %all-to-all-start.1 = ((bf16[64,128,128]{2,1,0:T(8,128)(2,1)}), bf16[64,128,128]{2,1,0:T(8,128)(2,1)S(1)}, u32[]{:S(2)}, u32[]{:S(2)}) async-start(bf16[64,128,128]{2,1,0:T(8,128)(2,1)} %param.6), calls=%async_computation.1 | async-start | bytes 4194304 | tf_op jit(solution)/shard_map/all_to_all | solution.py:19
  23.7 73.0 %all-gather.7.cloned.1.call-start = ((), (), s32[]{:S(2)}) async-start(), calls=%async_computation.6 | async-start | bytes 1179648 | tf_op jit(solution)/shard_map/all_gather | solution.py:38
  24.5 107.4 %reduce-scatter.5.cloned.1.call-start = ((), (), s32[]{:S(2)}) async-start(), calls=%async_computation.7 | async-start | bytes 1310720 | tf_op jit(solution)/shard_map/reduce_scatter | solution.py:44
  96.8 35.2 %copy-start.4 = (f32[256]{0:T(256)S(1)}, f32[256]{0:T(256)}, u32[]{:S(2)}) copy-start(f32[256]{0:T(256)} %param.10) | copy-start | bytes 3076
  101.5 110.9 %all-gather.11.cloned.1.call-start = ((), (), s32[]{:S(2)}) async-start(), calls=%async_computation.12 | async-start | bytes 8650752 | tf_op jit(solution)/shard_map/all_gather | solution.py:49
  134.3 111.2 %reduce-scatter.9.cloned.1.call-start = ((), (), s32[]{:S(2)}) async-start(), calls=%async_computation.10 | async-start | bytes 2359296 | tf_op jit(solution)/shard_map/reduce_scatter | solution.py:45
  149.2 163.1 %all-gather.9.cloned.1.call-start = ((), (), s32[]{:S(2)}) async-start(), calls=%async_computation.8 | async-start | bytes 1179648 | tf_op jit(solution)/shard_map/all_gather | solution.py:38
  212.4 4.0 copy-start.1
  291.4 53.2 %reduce-scatter.7.cloned.1.call-start = ((), (), s32[]{:S(2)}) async-start(), calls=%async_computation.9 | async-start | bytes 1310720 | tf_op jit(solution)/shard_map/reduce_scatter | solution.py:44
  317.0 108.1 %all-gather.13.cloned.1.call-start = ((), (), s32[]{:S(2)}) async-start(), calls=%async_computation.13 | async-start | bytes 8650752 | tf_op jit(solution)/shard_map/all_gather | solution.py:49
  346.9 111.4 %reduce-scatter.11.cloned.1.call-start = ((), (), s32[]{:S(2)}) async-start(), calls=%async_computation.11 | async-start | bytes 2359296 | tf_op jit(solution)/shard_map/reduce_scatter | solution.py:45
  425.1 4.8 copy-start.5
Sparse Core Ops, SparseCore 0:
  26.7 30.5 all-gather.6
  101.7 30.2 reduce-scatter.4
  135.4 77.0 all-gather.10
  214.6 30.8 reduce-scatter.8
  291.5 20.6 all-gather.8
  317.1 27.4 reduce-scatter.6
  348.0 77.0 all-gather.12
  427.4 30.8 reduce-scatter.10
